TPU v7x, 32 devices: a whole 2x2x4 slice. The times are simulated.
32 devices in a mesh: row: 16 (over z, y, x), col: 2 (over core).
Axes of the slice: x: 2, y: 2, z: 4, core: 2. Of those that a mesh axis runs over, the one named last changes fastest.
Arguments:
- flow_state: float32 [4, 128, 64, 1024], P(None, 'row', 'col'), may hold values from -6 to 6
- spacing: float32 [128], replicated, may hold values from 0.004 to 0.012
- diffusivity: float32 [4], replicated, may hold values from 0.03 to 0.1
Outputs:
- flow_next: float32 [4, 128, 64, 1024], P(None, 'row', 'col')
All inputs are finite; a program needn't handle non-finite values.
Results may differ from a plain program's by a relative error of at most 0.00023.
Values sent between devices are 32-bit elements; how exact they have to be, the bound alone decides.
A program may use at most 128 MiB of HBM per device.

v0:
```python
import functools

import jax
import jax.numpy as jnp
from jax import lax
from jax.experimental import pallas as pl
from jax.experimental.pallas import tpu as pltpu
from jax.sharding import PartitionSpec as P

time_step = 0.02
cell_width = 0.1
buoyancy = 1.0
UNROLL = 8
MESH = pl.DeviceIdType.MESH

LAM, RHO, MU, WIN, GEE, UPPER, QSH, DT_ACROSS, RATE, TABLES = range(10)


def moved(value, by):
    return pltpu.roll(value, by % value.shape[1], 1)


def pivots(low, upp, lane, sign):
    levels = low.shape[1]
    place = lane if sign == 1 else levels - 1 - lane
    one, zero = jnp.ones_like(low), jnp.zeros_like(low)
    before = jnp.where(place == 0, one, moved(upp, sign))
    a, b, c, d = one + low, before, one, before
    shift = 1
    while shift < levels:
        inside = place >= shift
        pa = jnp.where(inside, moved(a, sign * shift), one)
        pb = jnp.where(inside, moved(b, sign * shift), zero)
        pc = jnp.where(inside, moved(c, sign * shift), zero)
        pd = jnp.where(inside, moved(d, sign * shift), one)
        na, nb = a * pa + b * pc, a * pb + b * pd
        nc, nd = c * pa + d * pc, c * pb + d * pd
        scale = 1.0 / na
        a, b, c, d = na * scale, nb * scale, nc * scale, nd * scale
        shift *= 2
    g = a / c
    rho = 1.0 / (g + upp)
    return g, rho, g * rho, place


def fill_tables(width, thick, diff, tab):
    levels = thick.shape[1]
    lane = lax.broadcasted_iota(jnp.int32, (8, levels), 1)
    sub = lax.broadcasted_iota(jnp.int32, (8, levels), 0)
    comps = diff.shape[0]
    rate = jnp.zeros((8, levels), jnp.float32)
    for c in range(comps):
        rate = jnp.where(sub % comps == c, (2.0 * time_step) * diff[c], rate)
    below = jnp.broadcast_to(thick[...], (8, levels))
    above = jnp.where(lane == levels - 1, below, moved(below, -1))
    across = below + above
    low = rate / (across * below)
    upp = rate / (across * above)
    tables = {}
    for sign, first, second in ((1, low, upp), (-1, upp, low)):
        g, rho, ratio, place = pivots(first, second, lane, sign)
        lam = jnp.where(place == 0, 0.0, first * moved(rho, sign))
        window = lam
        for step in range(1, width):
            window = window * moved(lam, sign * step)
        ahead = jnp.where(place == 0, 1.0, moved(ratio, sign))
        tables[sign] = (lam, rho, second * rho, window, g, second, ahead)
    for index in range(QSH + 1):
        tab[index] = jnp.where(sub < comps, tables[1][index], tables[-1][index])
    tab[DT_ACROSS] = time_step / across
    tab[RATE] = rate


def step_kernel(
    rows, cols, group, state, spacing, diffusivity, out, q, thick, diff, vtab, tab, ysend, yrecv,
    wrecv, ploc, dup, tot, be, got, top, ztop, ret, pq, load, small, ysem, wsem, s1, s2, s3,
):
    comps, depth, ny, nx = q.shape
    levels = rows * depth
    count = rows // group
    piece = nx // group
    me, col = lax.axis_index("row"), lax.axis_index("col")
    z, g = me // group, me % group
    base = me * depth
    nxt, prv = (col + 1) % cols, (col + cols - 1) % cols

    loads = [
        pltpu.make_async_copy(state.at[c], q.at[c], load.at[c]) for c in range(comps)
    ]
    takes = [
        pltpu.make_async_copy(spacing, thick, small.at[0]),
        pltpu.make_async_copy(diffusivity, diff, small.at[1]),
    ]
    for copy in loads + takes:
        copy.start()

    barrier = pltpu.get_barrier_semaphore()
    for o in range(1, rows):
        pl.semaphore_signal(
            barrier, inc=1, device_id=((me + o) % rows, col), device_id_type=MESH
        )
    sides = [nxt] if cols == 2 else [nxt, prv]
    for side in sides:
        pl.semaphore_signal(barrier, inc=1, device_id=(me, side), device_id_type=MESH)
    def remote(src, dst, sems, index, device):
        return pltpu.make_async_remote_copy(
            src_ref=src,
            dst_ref=dst,
            send_sem=sems.at[(0, *index)],
            recv_sem=sems.at[(1, *index)],
            device_id=device,
            device_id_type=MESH,
        )

    w_down = remote(
        state.at[2, 0], wrecv.at[1], wsem, (1,), (jnp.maximum(me - 1, 0), col)
    )
    w_up = remote(
        state.at[2, depth - 1], wrecv.at[0], wsem, (0,), (jnp.minimum(me + 1, rows - 1), col)
    )

    for copy in takes:
        copy.wait()
    fill_tables(depth, thick, diff, vtab)
    publish = pltpu.make_async_copy(vtab, tab, small.at[2])
    publish.start()

    def y_copies(c):
        return [
            remote(ysend.at[c, 0], yrecv.at[c, 0], ysem, (c, 0), (me, nxt)),
            remote(ysend.at[c, 1], yrecv.at[c, 1], ysem, (c, 1), (me, prv)),
        ]

    for c in range(comps):
        loads[c].wait()
        for k in range(depth):
            ysend[c, 0, k : k + 1, :] = q[c, k, ny - 1 : ny, :]
            ysend[c, 1, k : k + 1, :] = q[c, k, 0:1, :]

    pl.semaphore_wait(barrier, rows - 1 + len(sides))

    @pl.when(me > 0)
    def _():
        w_down.start()

    @pl.when(me < rows - 1)
    def _():
        w_up.start()

    for c in range(comps):
        for copy in y_copies(c):
            copy.start()

    @pl.when(me == 0)
    def _():
        wrecv[0] = jnp.zeros((ny, nx), jnp.float32)

    @pl.when(me == rows - 1)
    def _():
        wrecv[1] = jnp.zeros((ny, nx), jnp.float32)

    def up(table, c, level):
        return tab[table, c, jnp.clip(level, 0, levels - 1)]

    def down(table, c, level):
        return tab[table, comps + c, jnp.clip(level, 0, levels - 1)]

    publish.wait()
    slab = 8
    row_of = lax.broadcasted_iota(jnp.int32, (slab, nx), 0)
    half = time_step / (2.0 * cell_width)

    def peer(o):
        return (g + o) % group

    def push(c, o):
        to = peer(o)
        return remote(
            be.at[c, to], got.at[c, o], s1, (c, o), (z * group + to, col)
        )

    def send_z(c, o, way):
        to = z + o if way == 0 else z - o
        to = jnp.clip(to, 0, count - 1)
        return remote(
            top.at[c, way], ztop.at[c, way, o - 1], s2, (c, way, o - 1), (to * group + g, col)
        )

    def give(c, o):
        to = peer(o)
        return remote(
            ret.at[c, to], pq.at[c, g], s3, (c, o), (z * group + to, col)
        )

    def stencil(c):
        for copy in y_copies(c):
            copy.wait_recv()
        alpha = tab[RATE, c, 0] * (0.5 / cell_width**2)
        keep = 1.0 - 4.0 * alpha
        for r in range(0, ny, slab):

            def level(k, carry, c=c, r=r, alpha=alpha, keep=keep):
                below, total, beta = carry
                scale = up(DT_ACROSS, 0, base + k)
                c_up = jnp.where(k == depth - 1, 0.0, scale)
                c_dn = jnp.where(k == 0, 0.0, scale)
                here = pl.ds(r, slab)
                centre = q[c, k, here, :]
                x_left = pltpu.roll(centre, 1, 1)
                x_right = pltpu.roll(centre, nx - 1, 1)
                if r == 0:
                    first = yrecv[c, 0, pl.ds(k, 1), :]
                else:
                    first = q[c, k, r - 1 : r, :]
                if r + slab == ny:
                    last = yrecv[c, 1, pl.ds(k, 1), :]
                else:
                    last = q[c, k, r + slab : r + slab + 1, :]
                y_left = jnp.where(row_of == 0, first, pltpu.roll(centre, 1, 0))
                y_right = jnp.where(row_of == slab - 1, last, pltpu.roll(centre, slab - 1, 0))
                z_up = q[c, jnp.minimum(k + 1, depth - 1), here, :]
                z_dn = q[c, jnp.maximum(k - 1, 0), here, :]
                value = keep * centre + alpha * ((x_left + x_right) + (y_left + y_right))
                value = value - (half * q[0, k, here, :]) * (x_right - x_left)
                value = value - (half * q[1, k, here, :]) * (y_right - y_left)
                value = value - q[2, k, here, :] * (c_up * z_up - c_dn * z_dn)
                if c == 2:
                    value = value + (time_step * buoyancy) * q[3, k, here, :]
                if c == 3:
                    value = value + time_step * q[2, k, here, :]
                below = value + up(LAM, c, base + k) * below
                out[c, k, here, :] = below
                total = total + beta * value
                return below, total, beta * down(LAM, c, base + k)

            start = jnp.zeros((slab, nx), jnp.float32)
            _, total, _ = lax.fori_loop(
                0, depth, level, (start, start, down(LAM, c, base - 1)), unroll=min(depth, UNROLL)
            )
            tot[c, pl.ds(r, slab), :] = total

    def finish(c):
        beta = down(LAM, c, base - 1)
        for k in range(depth):
            beta = beta * down(LAM, c, base + k)
        pi = 1.0
        for k in range(1, depth):
            pi = pi * up(LAM, c, base + k)
        for r in range(0, ny, slab):
            here = pl.ds(r, slab)
            below, total = out[c, depth - 1, here, :], tot[c, here, :]
            d_up = up(DT_ACROSS, 0, base + depth) * (wrecv[1, here, :] * q[c, depth - 1, here, :])
            d_dn = -up(DT_ACROSS, 0, base - 1) * (wrecv[0, here, :] * q[c, 0, here, :])
            p_loc = up(LAM, c, base) * d_dn
            ploc[c, here, :] = p_loc
            dup[c, here, :] = down(LAM, c, base + depth - 1) * d_up
            b = up(LAM, c, base + depth) * (below + pi * p_loc) + d_up
            e = total + beta * d_up + d_dn
            for p in range(group):
                be[c, p, 0, here, :] = b[:, p * piece : (p + 1) * piece]
                be[c, p, 1, here, :] = e[:, p * piece : (p + 1) * piece]
        for o in range(1, group):
            push(c, o).start()
        got[c, 0] = be[c, g]

    for c in range(comps):
        stencil(c)
        if c == 1:

            @pl.when(me > 0)
            def _():
                w_up.wait_recv()

            @pl.when(me < rows - 1)
            def _():
                w_down.wait_recv()

            finish(0)
        if c >= 1:
            finish(c)

    def up_factor(c, j):
        return up(WIN, c, (j + 1) * depth)

    def down_factor(c, j):
        return down(WIN, c, j * depth - 1)

    def slot(other):
        return (g + group - other) % group

    for c in range(comps):
        for o in range(1, group):
            push(c, o).wait_recv()
        total = got[c, slot(0), 0]
        for j in range(1, group):
            total = got[c, slot(j), 0] + up_factor(c, z * group + j) * total
        top[c, 0] = total
        total = got[c, slot(group - 1), 1]
        for j in reversed(range(group - 1)):
            total = got[c, slot(j), 1] + down_factor(c, z * group + j) * total
        top[c, 1] = total
        for o in range(1, count):

            @pl.when(z + o < count)
            def _(c=c, o=o):
                send_z(c, o, 0).start()

            @pl.when(z - o >= 0)
            def _(c=c, o=o):
                send_z(c, o, 1).start()

    for c in range(comps):
        for way in range(2):
            acc = ret.at[c, 0, way]
            acc[...] = jnp.zeros((ny, piece), jnp.float32)
            weight = 1.0
            for o in range(1, count):
                source = z - o if way == 0 else z + o

                @pl.when((source >= 0) & (source < count))
                def _(c=c, o=o, way=way, weight=weight, acc=acc):
                    send_z(c, o, way).wait_recv()
                    acc[...] += weight * ztop[c, way, o - 1]

                for j in range(group):
                    device = source * group + j
                    weight = weight * (up_factor if way == 0 else down_factor)(c, device)
        carry = ret[c, 0, 0]
        for j in range(group):
            ret[c, j, 0] = carry
            if j < group - 1:
                carry = got[c, slot(j), 0] + up_factor(c, z * group + j) * carry
        carry = ret[c, 0, 1]
        for j in reversed(range(group)):
            ret[c, j, 1] = carry
            if j > 0:
                carry = got[c, slot(j), 1] + down_factor(c, z * group + j) * carry
        for o in range(1, group):
            give(c, o).start()
        pq[c, g] = ret[c, g]

    for c in range(comps):
        for o in range(1, group):
            source = (g + group - o) % group
            remote(
                ret.at[c, source], pq.at[c, source], s3, (c, o), (z * group + source, col)
            ).wait_recv()
        pis = [jnp.float32(1.0)]
        for k in range(1, depth):
            pis.append(pis[-1] * up(LAM, c, base + k))
        end = base + depth - 1
        den = up(GEE, c, end) + up(UPPER, c, end) * down(QSH, c, end)
        for p in range(group):
            span = pl.ds(p * piece, piece)
            carry = pq[c, p, 0] + ploc[c, :, span]
            x = out[c, depth - 1, :, span] + pis[-1] * carry
            x = (x + (pq[c, p, 1] + dup[c, :, span])) / den
            out[c, depth - 1, :, span] = x
            for k in reversed(range(depth - 1)):
                rho = up(RHO, c, base + k)
                x = rho * out[c, k, :, span] + (rho * pis[k]) * carry + up(MU, c, base + k) * x
                out[c, k, :, span] = x

    for c in range(comps):
        for copy in y_copies(c):
            copy.wait_send()

    @pl.when(me > 0)
    def _():
        w_down.wait_send()

    @pl.when(me < rows - 1)
    def _():
        w_up.wait_send()

    for c in range(comps):
        for o in range(1, group):
            push(c, o).wait_send()
            give(c, o).wait_send()
        for o in range(1, count):

            @pl.when(z + o < count)
            def _(c=c, o=o):
                send_z(c, o, 0).wait_send()

            @pl.when(z - o >= 0)
            def _(c=c, o=o):
                send_z(c, o, 1).wait_send()


def group_of(rows, nx):
    group = 1
    while group * group < rows and rows % (2 * group) == 0 and nx % (256 * group) == 0:
        group *= 2
    return group


def shards(rows, cols, flow_state, spacing, diffusivity):
    comps, depth, ny, nx = flow_state.shape
    group = group_of(rows, nx)
    count = rows // group
    piece = nx // group
    levels = spacing.shape[0]
    f32 = jnp.float32
    vmem = functools.partial(pltpu.VMEM, dtype=f32)
    dma = pltpu.SemaphoreType.DMA
    return pl.pallas_call(
        functools.partial(step_kernel, rows, cols, group),
        out_shape=jax.ShapeDtypeStruct(flow_state.shape, f32),
        in_specs=[pl.BlockSpec(memory_space=pltpu.HBM)] * 3,
        out_specs=pl.BlockSpec(memory_space=pltpu.VMEM),
        scratch_shapes=[
            vmem(flow_state.shape),
            vmem((1, levels)),
            pltpu.SMEM((comps,), f32),
            vmem((TABLES, 8, levels)),
            pltpu.SMEM((TABLES, 8, levels), f32),
            vmem((comps, 2, depth, nx)),
            vmem((comps, 2, depth, nx)),
            vmem((2, ny, nx)),
            vmem((comps, ny, nx)),
            vmem((comps, ny, nx)),
            vmem((comps, ny, nx)),
            vmem((comps, group, 2, ny, piece)),
            vmem((comps, group, 2, ny, piece)),
            vmem((comps, 2, ny, piece)),
            vmem((comps, 2, count - 1, ny, piece)),
            vmem((comps, group, 2, ny, piece)),
            vmem((comps, group, 2, ny, piece)),
            dma((comps,)),
            dma((3,)),
            dma((2, comps, 2)),
            dma((2, 2)),
            dma((2, comps, group)),
            dma((2, comps, 2, count - 1)),
            dma((2, comps, group)),
        ],
        compiler_params=pltpu.CompilerParams(
            collective_id=0, has_side_effects=True, vmem_limit_bytes=46 << 20
        ),
        name="convection_step",
    )(flow_state, spacing.reshape(1, levels), diffusivity)


def solution(mesh):
    rows, cols = mesh.shape["row"], mesh.shape["col"]
    placed = (P(None, "row", "col", None), P(), P())
    return jax.shard_map(
        functools.partial(shards, rows, cols),
        mesh=mesh,
        in_specs=placed,
        out_specs=P(None, "row", "col", None),
        check_vma=False,
    )
```

profile of v0, /device:TPU:0, one launch (start us, length us, event | category | flops | bytes accessed | tf_op | source)
XLA Modules:
  0.0 44.8 jit_solution(12397204143375670572)
XLA Ops:
  0.0 0.0 copy-start
  0.0 0.7 %copy-done = f32[128]{0:T(128)S(1)} copy-done((f32[128]{0:T(128)S(1)}, f32[128]{0:T(128)}, u32[]{:S(2)}) %copy-start) | copy-done | bytes 536
  0.7 0.0 copy-start.1
  0.7 0.7 %copy-done.1 = f32[4]{0:T(128)S(1)} copy-done((f32[4]{0:T(128)S(1)}, f32[4]{0:T(128)}, u32[]{:S(2)}) %copy-start.1) | copy-done | bytes 40
  1.3 41.5 %convection_step.1 = f32[4,8,32,1024]{3,2,1,0:T(8,128)S(1)} custom-call(f32[4,8,32,1024]{3,2,1,0:T(8,128)} %state.1, f32[1,128]{1,0:T(1,128)S(1)} %bitcast.1, f32[4]{0:T(128)S(1)} %copy-done.1), custom_call_target="tpu_custom_call" | custom-call | tf_op jit(solution)/shard_map/convection_step/pallas_call | solution.py:407
  42.8 2.0 %copy.5 = f32[4,8,32,1024]{3,2,1,0:T(8,128)} copy(f32[4,8,32,1024]{3,2,1,0:T(8,128)S(1)} %convection_step.1) | data formatting | bytes 8388608
Async XLA Ops:
  0.0 0.7 %copy-start = (f32[128]{0:T(128)S(1)}, f32[128]{0:T(128)}, u32[]{:S(2)}) copy-start(f32[128]{0:T(128)} %param.4) | copy-start | bytes 1540
  0.7 0.7 %copy-start.1 = (f32[4]{0:T(128)S(1)}, f32[4]{0:T(128)}, u32[]{:S(2)}) copy-start(f32[4]{0:T(128)} %diffusivity.1) | copy-start | bytes 52
where the time goes:
time: 44.9 us; the launch traced here: 44.8 us
  Pallas kernels  41.5 us (92%)
  local copies, waits for them, and re-layouts  3.33 us (7%)
    pallas_call x1, Pallas kernels, shards(): pl.pallas_call(functools.partial(step_kernel, rows, cols, group), out_sha...  41.5 us
    unnamed x5, local copies, waits for them, and re-layouts  3.33 us

commit v1 on v0

--- a/solution.py
+++ b/solution.py
@@ -439,7 +439,7 @@
             collective_id=0, has_side_effects=True, vmem_limit_bytes=46 << 20
         ),
         name="convection_step",
-    )(flow_state, spacing.reshape(1, levels), diffusivity)
+    )(flow_state, pltpu.with_memory_space_constraint(spacing.reshape(1, levels), pltpu.HBM), pltpu.with_memory_space_constraint(diffusivity, pltpu.HBM))
 
 
 def solution(mesh):

time: 44.9 us -> 43.6 us (0.971)
  local copies, waits for them, and re-layouts: 3.33 us -> 2.02 us
    unnamed x5 -> x1, local copies, waits for them, and re-layouts: 3.33 us -> 2.02 us
where the time goes in v1:
time: 43.6 us; the launch traced here: 43.5 us
  Pallas kernels  41.4 us (95%)
  local copies, waits for them, and re-layouts  2.02 us (5%)
    pallas_call x1, Pallas kernels, shards(): pl.pallas_call(functools.partial(step_kernel, rows, cols, group), out_sha...  41.4 us
    unnamed x1, local copies, waits for them, and re-layouts  2.02 us

profile of v1, /device:TPU:0, one launch (start us, length us, event | category | flops | bytes accessed | tf_op | source)
XLA Modules:
  0.0 43.5 jit_solution(2353124000291762216)
XLA Ops:
  0.0 41.4 %convection_step.1 = f32[4,8,32,1024]{3,2,1,0:T(8,128)S(1)} custom-call(f32[4,8,32,1024]{3,2,1,0:T(8,128)} %state.1, f32[1,128]{1,0:T(1,128)} %bitcast.1, f32[4]{0:T(128)} %diffusivity.1), custom_call_target="tpu_custom_call" | custom-call | tf_op jit(solution)/shard_map/convection_step/pallas_call | solution.py:407
  41.4 2.0 %copy.5 = f32[4,8,32,1024]{3,2,1,0:T(8,128)} copy(f32[4,8,32,1024]{3,2,1,0:T(8,128)S(1)} %convection_step.1) | data formatting | bytes 8388608

commit v2 on v1

--- a/solution.py
+++ b/solution.py
@@ -11,6 +11,8 @@
 cell_width = 0.1
 buoyancy = 1.0
 UNROLL = 8
+HALVES = 2
+LAG = 6
 MESH = pl.DeviceIdType.MESH
 
 LAM, RHO, MU, WIN, GEE, UPPER, QSH, DT_ACROSS, RATE, TABLES = range(10)
@@ -72,17 +74,20 @@
 
 
 def step_kernel(
-    rows, cols, group, state, spacing, diffusivity, out, q, thick, diff, vtab, tab, ysend, yrecv,
-    wrecv, ploc, dup, tot, be, got, top, ztop, ret, pq, load, small, ysem, wsem, s1, s2, s3,
+    rows, cols, group, halves, state, spacing, diffusivity, out, q, thick, diff, vtab, tab, ysend,
+    yrecv, wrecv, ploc, dup, tot, be, got, top, ztop, ret, pq, load, small, ready, ysem, wsem, s1,
+    s2, s3,
 ):
     comps, depth, ny, nx = q.shape
     levels = rows * depth
     count = rows // group
     piece = nx // group
+    part = ny // halves
     me, col = lax.axis_index("row"), lax.axis_index("col")
     z, g = me // group, me % group
     base = me * depth
     nxt, prv = (col + 1) % cols, (col + cols - 1) % cols
+    chunks = [(c, h) for h in range(halves) for c in range(comps)]
 
     loads = [
         pltpu.make_async_copy(state.at[c], q.at[c], load.at[c]) for c in range(comps)
@@ -91,17 +96,51 @@
         pltpu.make_async_copy(spacing, thick, small.at[0]),
         pltpu.make_async_copy(diffusivity, diff, small.at[1]),
     ]
-    for copy in loads + takes:
+    for copy in takes + loads:
         copy.start()
 
     barrier = pltpu.get_barrier_semaphore()
-    for o in range(1, rows):
-        pl.semaphore_signal(
-            barrier, inc=1, device_id=((me + o) % rows, col), device_id_type=MESH
-        )
-    sides = [nxt] if cols == 2 else [nxt, prv]
-    for side in sides:
-        pl.semaphore_signal(barrier, inc=1, device_id=(me, side), device_id_type=MESH)
+    ready_z, ready_w, ready_c = group, group + count, group + count + 1
+
+    def signal(sem, when, device):
+        @pl.when(when)
+        def _():
+            pl.semaphore_signal(sem, inc=1, device_id=device, device_id_type=MESH)
+
+    def await_ready(index, when):
+        @pl.when(when)
+        def _():
+            pl.semaphore_wait(ready.at[index], 1)
+
+    def peer(o):
+        return (g + o) % group
+
+    for o in range(1, group):
+        signal(barrier, g + o < group, (z * group + peer(o), col))
+    for o in range(1, count):
+        signal(barrier, z + o < count, (jnp.minimum(z + o, count - 1) * group + g, col))
+    signal(barrier, me < rows - 1, (jnp.minimum(me + 1, rows - 1), col))
+    signal(barrier, col < cols - 1, (me, nxt))
+    if cols > 2:
+        signal(barrier, col == 0, (me, prv))
+
+    earlier = g + z + jnp.minimum(me, 1) + jnp.minimum(col, 1)
+    if cols > 2:
+        earlier = earlier + col // (cols - 1)
+
+    @pl.when(earlier > 0)
+    def _():
+        pl.semaphore_wait(barrier, earlier)
+
+    signal(ready.at[ready_w], me > 0, (jnp.maximum(me - 1, 0), col))
+    signal(ready.at[ready_c], col > 0, (me, prv))
+    if cols > 2:
+        signal(ready.at[ready_c + 1], col == cols - 1, (me, nxt))
+    for o in range(1, group):
+        signal(ready.at[group - o], g + o >= group, (z * group + peer(o), col))
+    for o in range(1, count):
+        signal(ready.at[ready_z + o], z - o >= 0, (jnp.maximum(z - o, 0) * group + g, col))
+
     def remote(src, dst, sems, index, device):
         return pltpu.make_async_remote_copy(
             src_ref=src,
@@ -112,12 +151,34 @@
             device_id_type=MESH,
         )
 
-    w_down = remote(
-        state.at[2, 0], wrecv.at[1], wsem, (1,), (jnp.maximum(me - 1, 0), col)
-    )
-    w_up = remote(
-        state.at[2, depth - 1], wrecv.at[0], wsem, (0,), (jnp.minimum(me + 1, rows - 1), col)
-    )
+    def w_down(h):
+        here = pl.ds(h * part, part)
+        return remote(
+            state.at[2, 0, here], wrecv.at[1, here], wsem, (1, h), (jnp.maximum(me - 1, 0), col)
+        )
+
+    def w_up(h):
+        here = pl.ds(h * part, part)
+        return remote(
+            state.at[2, depth - 1, here],
+            wrecv.at[0, here],
+            wsem,
+            (0, h),
+            (jnp.minimum(me + 1, rows - 1), col),
+        )
+
+    for h in range(halves):
+
+        @pl.when(me > 0)
+        def _(h=h):
+            w_down(h).start()
+
+        if h == 0:
+            await_ready(ready_w, me < rows - 1)
+
+        @pl.when(me < rows - 1)
+        def _(h=h):
+            w_up(h).start()
 
     for copy in takes:
         copy.wait()
@@ -137,16 +198,9 @@
             ysend[c, 0, k : k + 1, :] = q[c, k, ny - 1 : ny, :]
             ysend[c, 1, k : k + 1, :] = q[c, k, 0:1, :]
 
-    pl.semaphore_wait(barrier, rows - 1 + len(sides))
-
-    @pl.when(me > 0)
-    def _():
-        w_down.start()
-
-    @pl.when(me < rows - 1)
-    def _():
-        w_up.start()
-
+    await_ready(ready_c, col < cols - 1)
+    if cols > 2:
+        await_ready(ready_c + 1, col == 0)
     for c in range(comps):
         for copy in y_copies(c):
             copy.start()
@@ -170,26 +224,29 @@
     row_of = lax.broadcasted_iota(jnp.int32, (slab, nx), 0)
     half = time_step / (2.0 * cell_width)
 
-    def peer(o):
-        return (g + o) % group
-
-    def push(c, o):
+    def push(i, o):
         to = peer(o)
         return remote(
-            be.at[c, to], got.at[c, o], s1, (c, o), (z * group + to, col)
-        )
-
-    def send_z(c, o, way):
+            be.at[i, to], got.at[i, o], s1, (i, o), (z * group + to, col)
+        )
+
+    def send_z(i, o, way):
         to = z + o if way == 0 else z - o
         to = jnp.clip(to, 0, count - 1)
         return remote(
-            top.at[c, way], ztop.at[c, way, o - 1], s2, (c, way, o - 1), (to * group + g, col)
-        )
-
-    def give(c, o):
+            top.at[i, way], ztop.at[i, way, o - 1], s2, (i, way, o - 1), (to * group + g, col)
+        )
+
+    def give(i, o):
         to = peer(o)
         return remote(
-            ret.at[c, to], pq.at[c, g], s3, (c, o), (z * group + to, col)
+            ret.at[i, to], pq.at[i, g], s3, (i, o), (z * group + to, col)
+        )
+
+    def given(i, o):
+        source = peer(group - o)
+        return remote(
+            ret.at[i, source], pq.at[i, source], s3, (i, o), (z * group + source, col)
         )
 
     def stencil(c):
@@ -239,15 +296,25 @@
             )
             tot[c, pl.ds(r, slab), :] = total
 
-    def finish(c):
+    def await_w(h):
+        @pl.when(me > 0)
+        def _():
+            w_up(h).wait_recv()
+
+        @pl.when(me < rows - 1)
+        def _():
+            w_down(h).wait_recv()
+
+    def finish(i):
+        c, h = chunks[i]
         beta = down(LAM, c, base - 1)
         for k in range(depth):
             beta = beta * down(LAM, c, base + k)
         pi = 1.0
         for k in range(1, depth):
             pi = pi * up(LAM, c, base + k)
-        for r in range(0, ny, slab):
-            here = pl.ds(r, slab)
+        for r in range(0, part, slab):
+            here, local = pl.ds(h * part + r, slab), pl.ds(r, slab)
             below, total = out[c, depth - 1, here, :], tot[c, here, :]
             d_up = up(DT_ACROSS, 0, base + depth) * (wrecv[1, here, :] * q[c, depth - 1, here, :])
             d_dn = -up(DT_ACROSS, 0, base - 1) * (wrecv[0, here, :] * q[c, 0, here, :])
@@ -257,27 +324,26 @@
             b = up(LAM, c, base + depth) * (below + pi * p_loc) + d_up
             e = total + beta * d_up + d_dn
             for p in range(group):
-                be[c, p, 0, here, :] = b[:, p * piece : (p + 1) * piece]
-                be[c, p, 1, here, :] = e[:, p * piece : (p + 1) * piece]
+                be[i, p, 0, local, :] = b[:, p * piece : (p + 1) * piece]
+                be[i, p, 1, local, :] = e[:, p * piece : (p + 1) * piece]
         for o in range(1, group):
-            push(c, o).start()
-        got[c, 0] = be[c, g]
+            if i == 0:
+                await_ready(o, g + o < group)
+            push(i, o).start()
+        got[i, 0] = be[i, g]
 
     for c in range(comps):
         stencil(c)
-        if c == 1:
-
-            @pl.when(me > 0)
-            def _():
-                w_up.wait_recv()
-
-            @pl.when(me < rows - 1)
-            def _():
-                w_down.wait_recv()
-
-            finish(0)
+        if c == min(1, comps - 1):
+            await_w(0)
+            for i in range(c):
+                finish(i)
         if c >= 1:
             finish(c)
+    for i in range(comps, len(chunks)):
+        if i % comps == 0:
+            await_w(i // comps)
+        finish(i)
 
     def up_factor(c, j):
         return up(WIN, c, (j + 1) * depth)
@@ -288,104 +354,120 @@
     def slot(other):
         return (g + group - other) % group
 
-    for c in range(comps):
+    def gather(i):
+        c = chunks[i][0]
         for o in range(1, group):
-            push(c, o).wait_recv()
-        total = got[c, slot(0), 0]
+            push(i, o).wait_recv()
+        total = got[i, slot(0), 0]
         for j in range(1, group):
-            total = got[c, slot(j), 0] + up_factor(c, z * group + j) * total
-        top[c, 0] = total
-        total = got[c, slot(group - 1), 1]
+            total = got[i, slot(j), 0] + up_factor(c, z * group + j) * total
+        top[i, 0] = total
+        total = got[i, slot(group - 1), 1]
         for j in reversed(range(group - 1)):
-            total = got[c, slot(j), 1] + down_factor(c, z * group + j) * total
-        top[c, 1] = total
+            total = got[i, slot(j), 1] + down_factor(c, z * group + j) * total
+        top[i, 1] = total
         for o in range(1, count):
+            if i == 0:
+                await_ready(ready_z + o, z + o < count)
 
             @pl.when(z + o < count)
-            def _(c=c, o=o):
-                send_z(c, o, 0).start()
+            def _(o=o):
+                send_z(i, o, 0).start()
 
             @pl.when(z - o >= 0)
-            def _(c=c, o=o):
-                send_z(c, o, 1).start()
-
-    for c in range(comps):
+            def _(o=o):
+                send_z(i, o, 1).start()
+
+    def scatter(i):
+        c = chunks[i][0]
         for way in range(2):
-            acc = ret.at[c, 0, way]
-            acc[...] = jnp.zeros((ny, piece), jnp.float32)
+            acc = ret.at[i, 0, way]
+            acc[...] = jnp.zeros((part, piece), jnp.float32)
             weight = 1.0
             for o in range(1, count):
                 source = z - o if way == 0 else z + o
 
                 @pl.when((source >= 0) & (source < count))
-                def _(c=c, o=o, way=way, weight=weight, acc=acc):
-                    send_z(c, o, way).wait_recv()
-                    acc[...] += weight * ztop[c, way, o - 1]
+                def _(o=o, way=way, weight=weight, acc=acc):
+                    send_z(i, o, way).wait_recv()
+                    acc[...] += weight * ztop[i, way, o - 1]
 
                 for j in range(group):
                     device = source * group + j
                     weight = weight * (up_factor if way == 0 else down_factor)(c, device)
-        carry = ret[c, 0, 0]
+        carry = ret[i, 0, 0]
         for j in range(group):
-            ret[c, j, 0] = carry
+            ret[i, j, 0] = carry
             if j < group - 1:
-                carry = got[c, slot(j), 0] + up_factor(c, z * group + j) * carry
-        carry = ret[c, 0, 1]
+                carry = got[i, slot(j), 0] + up_factor(c, z * group + j) * carry
+        carry = ret[i, 0, 1]
         for j in reversed(range(group)):
-            ret[c, j, 1] = carry
+            ret[i, j, 1] = carry
             if j > 0:
-                carry = got[c, slot(j), 1] + down_factor(c, z * group + j) * carry
+                carry = got[i, slot(j), 1] + down_factor(c, z * group + j) * carry
         for o in range(1, group):
-            give(c, o).start()
-        pq[c, g] = ret[c, g]
-
-    for c in range(comps):
-        for o in range(1, group):
-            source = (g + group - o) % group
-            remote(
-                ret.at[c, source], pq.at[c, source], s3, (c, o), (z * group + source, col)
-            ).wait_recv()
+            give(i, o).start()
+        pq[i, g] = ret[i, g]
+
+    def settle(i):
+        c, h = chunks[i]
+        here = pl.ds(h * part, part)
         pis = [jnp.float32(1.0)]
         for k in range(1, depth):
             pis.append(pis[-1] * up(LAM, c, base + k))
         end = base + depth - 1
         den = up(GEE, c, end) + up(UPPER, c, end) * down(QSH, c, end)
-        for p in range(group):
-            span = pl.ds(p * piece, piece)
-            carry = pq[c, p, 0] + ploc[c, :, span]
-            x = out[c, depth - 1, :, span] + pis[-1] * carry
-            x = (x + (pq[c, p, 1] + dup[c, :, span])) / den
-            out[c, depth - 1, :, span] = x
+        for o in range(group):
+            p = peer(group - o)
+            if o:
+                given(i, o).wait_recv()
+            span = pl.ds(pl.multiple_of(p * piece, piece), piece)
+            carry = pq[i, p, 0] + ploc[c, here, span]
+            x = out[c, depth - 1, here, span] + pis[-1] * carry
+            x = (x + (pq[i, p, 1] + dup[c, here, span])) / den
+            out[c, depth - 1, here, span] = x
             for k in reversed(range(depth - 1)):
                 rho = up(RHO, c, base + k)
-                x = rho * out[c, k, :, span] + (rho * pis[k]) * carry + up(MU, c, base + k) * x
-                out[c, k, :, span] = x
+                x = rho * out[c, k, here, span] + (rho * pis[k]) * carry + up(MU, c, base + k) * x
+                out[c, k, here, span] = x
+
+    total_chunks = len(chunks)
+    for i in range(total_chunks):
+        gather(i)
+        if i >= LAG:
+            scatter(i - LAG)
+    for i in range(max(total_chunks - LAG, 0), total_chunks):
+        scatter(i)
+    for i in range(total_chunks):
+        settle(i)
 
     for c in range(comps):
         for copy in y_copies(c):
             copy.wait_send()
 
-    @pl.when(me > 0)
-    def _():
-        w_down.wait_send()
-
-    @pl.when(me < rows - 1)
-    def _():
-        w_up.wait_send()
-
-    for c in range(comps):
+    for h in range(halves):
+
+        @pl.when(me > 0)
+        def _(h=h):
+            w_down(h).wait_send()
+
+        @pl.when(me < rows - 1)
+        def _(h=h):
+            w_up(h).wait_send()
+
+    for i in range(total_chunks):
         for o in range(1, group):
-            push(c, o).wait_send()
-            give(c, o).wait_send()
+            push(i, o).wait_send()
+            give(i, o).wait_send()
         for o in range(1, count):
 
             @pl.when(z + o < count)
-            def _(c=c, o=o):
-                send_z(c, o, 0).wait_send()
+            def _(i=i, o=o):
+                send_z(i, o, 0).wait_send()
 
             @pl.when(z - o >= 0)
-            def _(c=c, o=o):
-                send_z(c, o, 1).wait_send()
+            def _(i=i, o=o):
+                send_z(i, o, 1).wait_send()
 
 
 def group_of(rows, nx):
@@ -400,12 +482,17 @@
     group = group_of(rows, nx)
     count = rows // group
     piece = nx // group
+    halves = HALVES if ny % (8 * HALVES) == 0 else 1
+    part = ny // halves
+    chunks = comps * halves
     levels = spacing.shape[0]
     f32 = jnp.float32
     vmem = functools.partial(pltpu.VMEM, dtype=f32)
     dma = pltpu.SemaphoreType.DMA
+    spacing = pltpu.with_memory_space_constraint(spacing.reshape(1, levels), pltpu.HBM)
+    diffusivity = pltpu.with_memory_space_constraint(diffusivity, pltpu.HBM)
     return pl.pallas_call(
-        functools.partial(step_kernel, rows, cols, group),
+        functools.partial(step_kernel, rows, cols, group, halves),
         out_shape=jax.ShapeDtypeStruct(flow_state.shape, f32),
         in_specs=[pl.BlockSpec(memory_space=pltpu.HBM)] * 3,
         out_specs=pl.BlockSpec(memory_space=pltpu.VMEM),
@@ -421,25 +508,26 @@
             vmem((comps, ny, nx)),
             vmem((comps, ny, nx)),
             vmem((comps, ny, nx)),
-            vmem((comps, group, 2, ny, piece)),
-            vmem((comps, group, 2, ny, piece)),
-            vmem((comps, 2, ny, piece)),
-            vmem((comps, 2, count - 1, ny, piece)),
-            vmem((comps, group, 2, ny, piece)),
-            vmem((comps, group, 2, ny, piece)),
+            vmem((chunks, group, 2, part, piece)),
+            vmem((chunks, group, 2, part, piece)),
+            vmem((chunks, 2, part, piece)),
+            vmem((chunks, 2, max(count - 1, 1), part, piece)),
+            vmem((chunks, group, 2, part, piece)),
+            vmem((chunks, group, 2, part, piece)),
             dma((comps,)),
             dma((3,)),
+            pltpu.SemaphoreType.REGULAR((group + count + 3,)),
             dma((2, comps, 2)),
-            dma((2, 2)),
-            dma((2, comps, group)),
-            dma((2, comps, 2, count - 1)),
-            dma((2, comps, group)),
+            dma((2, 2, halves)),
+            dma((2, chunks, group)),
+            dma((2, chunks, 2, max(count - 1, 1))),
+            dma((2, chunks, group)),
         ],
         compiler_params=pltpu.CompilerParams(
             collective_id=0, has_side_effects=True, vmem_limit_bytes=46 << 20
         ),
         name="convection_step",
-    )(flow_state, pltpu.with_memory_space_constraint(spacing.reshape(1, levels), pltpu.HBM), pltpu.with_memory_space_constraint(diffusivity, pltpu.HBM))
+    )(flow_state, spacing, diffusivity)
 
 
 def solution(mesh):

time: 43.6 us -> 40.2 us (0.922)
  Pallas kernels: 41.4 us -> 38 us
    pallas_call x1, Pallas kernels: 41.4 us -> 38 us  [shards(): pl.pallas_call(functools.partial(step_kernel, rows, cols, group, halves),...]
where the time goes in v2:
time: 40.2 us; the launch traced here: 40 us
  Pallas kernels  38 us (95%)
  local copies, waits for them, and re-layouts  2.02 us (5%)
    pallas_call x1, Pallas kernels, shards(): pl.pallas_call(functools.partial(step_kernel, rows, cols, group, halves),...  38 us
    unnamed x1, local copies, waits for them, and re-layouts  2.02 us

profile of v2, /device:TPU:0, one launch (start us, length us, event | category | flops | bytes accessed | tf_op | source)
XLA Modules:
  0.0 40.0 jit_solution(6457786863849809621)
XLA Ops:
  0.0 38.0 %convection_step.1 = f32[4,8,32,1024]{3,2,1,0:T(8,128)S(1)} custom-call(f32[4,8,32,1024]{3,2,1,0:T(8,128)} %state.1, f32[1,128]{1,0:T(1,128)} %bitcast.1, f32[4]{0:T(128)} %diffusivity.1), custom_call_target="tpu_custom_call" | custom-call | tf_op jit(solution)/shard_map/convection_step/pallas_call | solution.py:494
  38.0 2.0 %copy.5 = f32[4,8,32,1024]{3,2,1,0:T(8,128)} copy(f32[4,8,32,1024]{3,2,1,0:T(8,128)S(1)} %convection_step.1) | data formatting | bytes 8388608

commit v3 on v2

--- a/solution.py
+++ b/solution.py
@@ -15,6 +15,7 @@
 LAG = 6
 MESH = pl.DeviceIdType.MESH
 
+PUSH, ALONG_Z, GIVE, Y_ROWS, W_UP, W_DOWN = range(6)
 LAM, RHO, MU, WIN, GEE, UPPER, QSH, DT_ACROSS, RATE, TABLES = range(10)
 
 
@@ -75,8 +76,8 @@
 
 def step_kernel(
     rows, cols, group, halves, state, spacing, diffusivity, out, q, thick, diff, vtab, tab, ysend,
-    yrecv, wrecv, ploc, dup, tot, be, got, top, ztop, ret, pq, load, small, ready, ysem, wsem, s1,
-    s2, s3,
+    yrecv, wrecv, ploc, dup, tot, be, got, top, ztop, ret, pq, small, ready, sent, load, ysem, wsem,
+    s1, s2, s3,
 ):
     comps, depth, ny, nx = q.shape
     levels = rows * depth
@@ -89,9 +90,7 @@
     nxt, prv = (col + 1) % cols, (col + cols - 1) % cols
     chunks = [(c, h) for h in range(halves) for c in range(comps)]
 
-    loads = [
-        pltpu.make_async_copy(state.at[c], q.at[c], load.at[c]) for c in range(comps)
-    ]
+    loads = [pltpu.make_async_copy(state, q, load)]
     takes = [
         pltpu.make_async_copy(spacing, thick, small.at[0]),
         pltpu.make_async_copy(diffusivity, diff, small.at[1]),
@@ -100,61 +99,58 @@
         copy.start()
 
     barrier = pltpu.get_barrier_semaphore()
-    ready_z, ready_w, ready_c = group, group + count, group + count + 1
 
     def signal(sem, when, device):
         @pl.when(when)
         def _():
             pl.semaphore_signal(sem, inc=1, device_id=device, device_id_type=MESH)
 
-    def await_ready(index, when):
+    def greet(device):
+        pl.semaphore_signal(barrier, inc=1, device_id=device, device_id_type=MESH)
+
+    def await_ready(o, when):
         @pl.when(when)
         def _():
-            pl.semaphore_wait(ready.at[index], 1)
+            pl.semaphore_wait(ready.at[o - 1], 1)
 
     def peer(o):
         return (g + o) % group
 
+    signal(barrier, me > 0, (jnp.maximum(me - 1, 0), col))
+    signal(barrier, me < rows - 1, (jnp.minimum(me + 1, rows - 1), col))
     for o in range(1, group):
-        signal(barrier, g + o < group, (z * group + peer(o), col))
+        greet((z * group + peer(o), col))
+    sides = [nxt] if cols == 2 else [nxt, prv]
+    for side in sides:
+        greet((me, side))
     for o in range(1, count):
         signal(barrier, z + o < count, (jnp.minimum(z + o, count - 1) * group + g, col))
-    signal(barrier, me < rows - 1, (jnp.minimum(me + 1, rows - 1), col))
-    signal(barrier, col < cols - 1, (me, nxt))
-    if cols > 2:
-        signal(barrier, col == 0, (me, prv))
-
-    earlier = g + z + jnp.minimum(me, 1) + jnp.minimum(col, 1)
-    if cols > 2:
-        earlier = earlier + col // (cols - 1)
-
-    @pl.when(earlier > 0)
-    def _():
-        pl.semaphore_wait(barrier, earlier)
-
-    signal(ready.at[ready_w], me > 0, (jnp.maximum(me - 1, 0), col))
-    signal(ready.at[ready_c], col > 0, (me, prv))
-    if cols > 2:
-        signal(ready.at[ready_c + 1], col == cols - 1, (me, nxt))
-    for o in range(1, group):
-        signal(ready.at[group - o], g + o >= group, (z * group + peer(o), col))
-    for o in range(1, count):
-        signal(ready.at[ready_z + o], z - o >= 0, (jnp.maximum(z - o, 0) * group + g, col))
-
-    def remote(src, dst, sems, index, device):
+    greetings = group - 1 + len(sides) + z
+    greetings = greetings + jnp.minimum(me, 1) + jnp.minimum(rows - 1 - me, 1)
+
+    pl.semaphore_wait(barrier, greetings)
+
+    def remote(src, dst, kind, sem, device):
         return pltpu.make_async_remote_copy(
             src_ref=src,
             dst_ref=dst,
-            send_sem=sems.at[(0, *index)],
-            recv_sem=sems.at[(1, *index)],
+            send_sem=sent.at[kind],
+            recv_sem=sem,
             device_id=device,
             device_id_type=MESH,
         )
 
+    def await_bytes(ref, sem):
+        pltpu.make_async_copy(ref, ref, sem).wait()
+
     def w_down(h):
         here = pl.ds(h * part, part)
         return remote(
-            state.at[2, 0, here], wrecv.at[1, here], wsem, (1, h), (jnp.maximum(me - 1, 0), col)
+            state.at[2, 0, here],
+            wrecv.at[1, here],
+            W_DOWN,
+            wsem.at[1, h],
+            (jnp.maximum(me - 1, 0), col),
         )
 
     def w_up(h):
@@ -162,8 +158,8 @@
         return remote(
             state.at[2, depth - 1, here],
             wrecv.at[0, here],
-            wsem,
-            (0, h),
+            W_UP,
+            wsem.at[0, h],
             (jnp.minimum(me + 1, rows - 1), col),
         )
 
@@ -173,12 +169,12 @@
         def _(h=h):
             w_down(h).start()
 
-        if h == 0:
-            await_ready(ready_w, me < rows - 1)
-
         @pl.when(me < rows - 1)
         def _(h=h):
             w_up(h).start()
+
+    for o in range(1, count):
+        signal(ready.at[o - 1], z - o >= 0, (jnp.maximum(z - o, 0) * group + g, col))
 
     for copy in takes:
         copy.wait()
@@ -188,19 +184,16 @@
 
     def y_copies(c):
         return [
-            remote(ysend.at[c, 0], yrecv.at[c, 0], ysem, (c, 0), (me, nxt)),
-            remote(ysend.at[c, 1], yrecv.at[c, 1], ysem, (c, 1), (me, prv)),
+            remote(ysend.at[c, 0], yrecv.at[c, 0], Y_ROWS, ysem, (me, nxt)),
+            remote(ysend.at[c, 1], yrecv.at[c, 1], Y_ROWS, ysem, (me, prv)),
         ]
 
+    loads[0].wait()
     for c in range(comps):
-        loads[c].wait()
         for k in range(depth):
             ysend[c, 0, k : k + 1, :] = q[c, k, ny - 1 : ny, :]
             ysend[c, 1, k : k + 1, :] = q[c, k, 0:1, :]
 
-    await_ready(ready_c, col < cols - 1)
-    if cols > 2:
-        await_ready(ready_c + 1, col == 0)
     for c in range(comps):
         for copy in y_copies(c):
             copy.start()
@@ -226,32 +219,23 @@
 
     def push(i, o):
         to = peer(o)
-        return remote(
-            be.at[i, to], got.at[i, o], s1, (i, o), (z * group + to, col)
-        )
+        return remote(be.at[i, to], got.at[i, o], PUSH, s1.at[i], (z * group + to, col))
 
     def send_z(i, o, way):
         to = z + o if way == 0 else z - o
         to = jnp.clip(to, 0, count - 1)
         return remote(
-            top.at[i, way], ztop.at[i, way, o - 1], s2, (i, way, o - 1), (to * group + g, col)
+            top.at[i, way], ztop.at[i, z_slot(o, way)], ALONG_Z, s2.at[i], (to * group + g, col)
         )
+
+    def z_slot(o, way):
+        return count - o - 1 if way == 0 else o - 1
 
     def give(i, o):
         to = peer(o)
-        return remote(
-            ret.at[i, to], pq.at[i, g], s3, (i, o), (z * group + to, col)
-        )
-
-    def given(i, o):
-        source = peer(group - o)
-        return remote(
-            ret.at[i, source], pq.at[i, source], s3, (i, o), (z * group + source, col)
-        )
+        return remote(ret.at[i, to], pq.at[i, group - o], GIVE, s3.at[i], (z * group + to, col))
 
     def stencil(c):
-        for copy in y_copies(c):
-            copy.wait_recv()
         alpha = tab[RATE, c, 0] * (0.5 / cell_width**2)
         keep = 1.0 - 4.0 * alpha
         for r in range(0, ny, slab):
@@ -327,11 +311,10 @@
                 be[i, p, 0, local, :] = b[:, p * piece : (p + 1) * piece]
                 be[i, p, 1, local, :] = e[:, p * piece : (p + 1) * piece]
         for o in range(1, group):
-            if i == 0:
-                await_ready(o, g + o < group)
             push(i, o).start()
         got[i, 0] = be[i, g]
 
+    await_bytes(yrecv, ysem)
     for c in range(comps):
         stencil(c)
         if c == min(1, comps - 1):
@@ -356,8 +339,8 @@
 
     def gather(i):
         c = chunks[i][0]
-        for o in range(1, group):
-            push(i, o).wait_recv()
+        if group > 1:
+            await_bytes(got.at[i, pl.ds(1, group - 1)], s1.at[i])
         total = got[i, slot(0), 0]
         for j in range(1, group):
             total = got[i, slot(j), 0] + up_factor(c, z * group + j) * total
@@ -368,7 +351,7 @@
         top[i, 1] = total
         for o in range(1, count):
             if i == 0:
-                await_ready(ready_z + o, z + o < count)
+                await_ready(o, z + o < count)
 
             @pl.when(z + o < count)
             def _(o=o):
@@ -380,6 +363,8 @@
 
     def scatter(i):
         c = chunks[i][0]
+        if count > 1:
+            await_bytes(ztop.at[i], s2.at[i])
         for way in range(2):
             acc = ret.at[i, 0, way]
             acc[...] = jnp.zeros((part, piece), jnp.float32)
@@ -389,8 +374,7 @@
 
                 @pl.when((source >= 0) & (source < count))
                 def _(o=o, way=way, weight=weight, acc=acc):
-                    send_z(i, o, way).wait_recv()
-                    acc[...] += weight * ztop[i, way, o - 1]
+                    acc[...] += weight * ztop[i, z_slot(o, way)]
 
                 for j in range(group):
                     device = source * group + j
@@ -407,7 +391,7 @@
                 carry = got[i, slot(j), 1] + down_factor(c, z * group + j) * carry
         for o in range(1, group):
             give(i, o).start()
-        pq[i, g] = ret[i, g]
+        pq[i, 0] = ret[i, g]
 
     def settle(i):
         c, h = chunks[i]
@@ -417,14 +401,14 @@
             pis.append(pis[-1] * up(LAM, c, base + k))
         end = base + depth - 1
         den = up(GEE, c, end) + up(UPPER, c, end) * down(QSH, c, end)
+        if group > 1:
+            await_bytes(pq.at[i, pl.ds(1, group - 1)], s3.at[i])
         for o in range(group):
-            p = peer(group - o)
-            if o:
-                given(i, o).wait_recv()
+            p = peer(o)
             span = pl.ds(pl.multiple_of(p * piece, piece), piece)
-            carry = pq[i, p, 0] + ploc[c, here, span]
+            carry = pq[i, o, 0] + ploc[c, here, span]
             x = out[c, depth - 1, here, span] + pis[-1] * carry
-            x = (x + (pq[i, p, 1] + dup[c, here, span])) / den
+            x = (x + (pq[i, o, 1] + dup[c, here, span])) / den
             out[c, depth - 1, here, span] = x
             for k in reversed(range(depth - 1)):
                 rho = up(RHO, c, base + k)
@@ -441,33 +425,21 @@
     for i in range(total_chunks):
         settle(i)
 
-    for c in range(comps):
-        for copy in y_copies(c):
-            copy.wait_send()
-
-    for h in range(halves):
-
-        @pl.when(me > 0)
-        def _(h=h):
-            w_down(h).wait_send()
-
-        @pl.when(me < rows - 1)
-        def _(h=h):
-            w_up(h).wait_send()
-
-    for i in range(total_chunks):
-        for o in range(1, group):
-            push(i, o).wait_send()
-            give(i, o).wait_send()
-        for o in range(1, count):
-
-            @pl.when(z + o < count)
-            def _(i=i, o=o):
-                send_z(i, o, 0).wait_send()
-
-            @pl.when(z - o >= 0)
-            def _(i=i, o=o):
-                send_z(i, o, 1).wait_send()
+    await_bytes(ysend, sent.at[Y_ROWS])
+
+    @pl.when(me > 0)
+    def _():
+        await_bytes(wrecv.at[0], sent.at[W_DOWN])
+
+    @pl.when(me < rows - 1)
+    def _():
+        await_bytes(wrecv.at[0], sent.at[W_UP])
+
+    if group > 1:
+        await_bytes(be.at[:, pl.ds(1, group - 1)], sent.at[PUSH])
+        await_bytes(ret.at[:, pl.ds(1, group - 1)], sent.at[GIVE])
+    if count > 1:
+        await_bytes(ztop, sent.at[ALONG_Z])
 
 
 def group_of(rows, nx):
@@ -511,17 +483,18 @@
             vmem((chunks, group, 2, part, piece)),
             vmem((chunks, group, 2, part, piece)),
             vmem((chunks, 2, part, piece)),
-            vmem((chunks, 2, max(count - 1, 1), part, piece)),
+            vmem((chunks, max(count - 1, 1), part, piece)),
             vmem((chunks, group, 2, part, piece)),
             vmem((chunks, group, 2, part, piece)),
-            dma((comps,)),
             dma((3,)),
-            pltpu.SemaphoreType.REGULAR((group + count + 3,)),
-            dma((2, comps, 2)),
-            dma((2, 2, halves)),
-            dma((2, chunks, group)),
-            dma((2, chunks, 2, max(count - 1, 1))),
-            dma((2, chunks, group)),
+            pltpu.SemaphoreType.REGULAR((max(count - 1, 1),)),
+            dma((6,)),
+            dma,
+            dma,
+            dma((2, halves)),
+            dma((chunks,)),
+            dma((chunks,)),
+            dma((chunks,)),
         ],
         compiler_params=pltpu.CompilerParams(
             collective_id=0, has_side_effects=True, vmem_limit_bytes=46 << 20

time: 40.2 us -> 37.4 us (0.930)
  Pallas kernels: 38 us -> 35.3 us
    pallas_call x1, Pallas kernels: 38 us -> 35.3 us  [shards(): pl.pallas_call(functools.partial(step_kernel, rows, cols, group, halves),...]
where the time goes in v3:
time: 37.4 us; the launch traced here: 37.3 us
  Pallas kernels  35.3 us (94%)
  local copies, waits for them, and re-layouts  2.02 us (5%)
    pallas_call x1, Pallas kernels, shards(): pl.pallas_call(functools.partial(step_kernel, rows, cols, group, halves),...  35.3 us
    unnamed x1, local copies, waits for them, and re-layouts  2.02 us

profile of v3, /device:TPU:0, one launch (start us, length us, event | category | flops | bytes accessed | tf_op | source)
XLA Modules:
  0.0 37.3 jit_solution(3383312944516864452)
XLA Ops:
  0.0 35.3 %convection_step.1 = f32[4,8,32,1024]{3,2,1,0:T(8,128)S(1)} custom-call(f32[4,8,32,1024]{3,2,1,0:T(8,128)} %state.1, f32[1,128]{1,0:T(1,128)} %bitcast.1, f32[4]{0:T(128)} %diffusivity.1), custom_call_target="tpu_custom_call" | custom-call | tf_op jit(solution)/shard_map/convection_step/pallas_call | solution.py:466
  35.3 2.0 %copy.5 = f32[4,8,32,1024]{3,2,1,0:T(8,128)} copy(f32[4,8,32,1024]{3,2,1,0:T(8,128)S(1)} %convection_step.1) | data formatting | bytes 8388608

commit v4 on v3

--- a/solution.py
+++ b/solution.py
@@ -12,7 +12,7 @@
 buoyancy = 1.0
 UNROLL = 8
 HALVES = 2
-LAG = 6
+LAG = 3
 MESH = pl.DeviceIdType.MESH
 
 PUSH, ALONG_Z, GIVE, Y_ROWS, W_UP, W_DOWN = range(6)
@@ -201,10 +201,14 @@
     @pl.when(me == 0)
     def _():
         wrecv[0] = jnp.zeros((ny, nx), jnp.float32)
+        for o in range(1, group):
+            pq[:, 2 * o] = jnp.zeros((len(chunks), part, piece), jnp.float32)
 
     @pl.when(me == rows - 1)
     def _():
         wrecv[1] = jnp.zeros((ny, nx), jnp.float32)
+        for o in range(1, group):
+            pq[:, 2 * o + 1] = jnp.zeros((len(chunks), part, piece), jnp.float32)
 
     def up(table, c, level):
         return tab[table, c, jnp.clip(level, 0, levels - 1)]
@@ -217,9 +221,16 @@
     row_of = lax.broadcasted_iota(jnp.int32, (slab, nx), 0)
     half = time_step / (2.0 * cell_width)
 
-    def push(i, o):
+    def push(i, o, way=None):
         to = peer(o)
-        return remote(be.at[i, to], got.at[i, o], PUSH, s1.at[i], (z * group + to, col))
+        first, size = (0, 2) if way is None else (way, 1)
+        return remote(
+            be.at[i, pl.ds(2 * to + first, size)],
+            got.at[i, pl.ds(2 * o + first, size)],
+            PUSH,
+            s1.at[i],
+            (z * group + to, col),
+        )
 
     def send_z(i, o, way):
         to = z + o if way == 0 else z - o
@@ -231,9 +242,49 @@
     def z_slot(o, way):
         return count - o - 1 if way == 0 else o - 1
 
-    def give(i, o):
+    def give(i, o, way=None):
         to = peer(o)
-        return remote(ret.at[i, to], pq.at[i, group - o], GIVE, s3.at[i], (z * group + to, col))
+        first, size = (0, 2) if way is None else (way, 1)
+        return remote(
+            ret.at[i, pl.ds(2 * to + first, size)],
+            pq.at[i, pl.ds(2 * (group - o) + first, size)],
+            GIVE,
+            s3.at[i],
+            (z * group + to, col),
+        )
+
+    def start_of(copies, row, outward):
+        @pl.when(row == 0)
+        def _():
+            copies(outward).start()
+
+        @pl.when(row == rows - 1)
+        def _():
+            copies(1 - outward).start()
+
+        @pl.when((row > 0) & (row < rows - 1))
+        def _():
+            copies(None).start()
+
+    at_edge = (me == 0) | (me == rows - 1)
+    lacking = jnp.where((z == 0) & (g > 0), 1, 0)
+    lacking = lacking + jnp.where((z == count - 1) & (g < group - 1), 1, 0)
+
+    def await_edge(refs, sem):
+        @pl.when(at_edge)
+        def _():
+            await_bytes(refs(group - 1), sem)
+
+        @pl.when(jnp.logical_not(at_edge))
+        def _():
+            await_bytes(refs(2 * (group - 1)), sem)
+
+    def await_lacking(refs, sem):
+        for lacks in range(2 if count > 1 else 3):
+
+            @pl.when(lacking == lacks)
+            def _(lacks=lacks):
+                await_bytes(refs(2 * (group - 1) - lacks), sem)
 
     def stencil(c):
         alpha = tab[RATE, c, 0] * (0.5 / cell_width**2)
@@ -308,11 +359,12 @@
             b = up(LAM, c, base + depth) * (below + pi * p_loc) + d_up
             e = total + beta * d_up + d_dn
             for p in range(group):
-                be[i, p, 0, local, :] = b[:, p * piece : (p + 1) * piece]
-                be[i, p, 1, local, :] = e[:, p * piece : (p + 1) * piece]
+                be[i, 2 * p, local, :] = b[:, p * piece : (p + 1) * piece]
+                be[i, 2 * p + 1, local, :] = e[:, p * piece : (p + 1) * piece]
         for o in range(1, group):
-            push(i, o).start()
-        got[i, 0] = be[i, g]
+            start_of(functools.partial(push, i, o), me, 0)
+        for way in range(2):
+            got[i, way] = be[i, 2 * g + way]
 
     await_bytes(yrecv, ysem)
     for c in range(comps):
@@ -340,15 +392,22 @@
     def gather(i):
         c = chunks[i][0]
         if group > 1:
-            await_bytes(got.at[i, pl.ds(1, group - 1)], s1.at[i])
-        total = got[i, slot(0), 0]
-        for j in range(1, group):
-            total = got[i, slot(j), 0] + up_factor(c, z * group + j) * total
-        top[i, 0] = total
-        total = got[i, slot(group - 1), 1]
-        for j in reversed(range(group - 1)):
-            total = got[i, slot(j), 1] + down_factor(c, z * group + j) * total
-        top[i, 1] = total
+            await_lacking(lambda size: got.at[i, pl.ds(2, size)], s1.at[i])
+
+        @pl.when(z < count - 1)
+        def _():
+            total = got[i, 2 * slot(0)]
+            for j in range(1, group):
+                total = got[i, 2 * slot(j)] + up_factor(c, z * group + j) * total
+            top[i, 0] = total
+
+        @pl.when(z > 0)
+        def _():
+            total = got[i, 2 * slot(group - 1) + 1]
+            for j in reversed(range(group - 1)):
+                total = got[i, 2 * slot(j) + 1] + down_factor(c, z * group + j) * total
+            top[i, 1] = total
+
         for o in range(1, count):
             if i == 0:
                 await_ready(o, z + o < count)
@@ -366,7 +425,7 @@
         if count > 1:
             await_bytes(ztop.at[i], s2.at[i])
         for way in range(2):
-            acc = ret.at[i, 0, way]
+            acc = ret.at[i, way]
             acc[...] = jnp.zeros((part, piece), jnp.float32)
             weight = 1.0
             for o in range(1, count):
@@ -379,19 +438,20 @@
                 for j in range(group):
                     device = source * group + j
                     weight = weight * (up_factor if way == 0 else down_factor)(c, device)
-        carry = ret[i, 0, 0]
+        carry = ret[i, 0]
         for j in range(group):
-            ret[i, j, 0] = carry
+            ret[i, 2 * j] = carry
             if j < group - 1:
-                carry = got[i, slot(j), 0] + up_factor(c, z * group + j) * carry
-        carry = ret[i, 0, 1]
+                carry = got[i, 2 * slot(j)] + up_factor(c, z * group + j) * carry
+        carry = ret[i, 1]
         for j in reversed(range(group)):
-            ret[i, j, 1] = carry
+            ret[i, 2 * j + 1] = carry
             if j > 0:
-                carry = got[i, slot(j), 1] + down_factor(c, z * group + j) * carry
+                carry = got[i, 2 * slot(j) + 1] + down_factor(c, z * group + j) * carry
         for o in range(1, group):
-            give(i, o).start()
-        pq[i, 0] = ret[i, g]
+            start_of(functools.partial(give, i, o), z * group + peer(o), 1)
+        for way in range(2):
+            pq[i, way] = ret[i, 2 * g + way]
 
     def settle(i):
         c, h = chunks[i]
@@ -402,13 +462,13 @@
         end = base + depth - 1
         den = up(GEE, c, end) + up(UPPER, c, end) * down(QSH, c, end)
         if group > 1:
-            await_bytes(pq.at[i, pl.ds(1, group - 1)], s3.at[i])
+            await_edge(lambda size: pq.at[i, pl.ds(0, size)], s3.at[i])
         for o in range(group):
             p = peer(o)
             span = pl.ds(pl.multiple_of(p * piece, piece), piece)
-            carry = pq[i, o, 0] + ploc[c, here, span]
+            carry = pq[i, 2 * o] + ploc[c, here, span]
             x = out[c, depth - 1, here, span] + pis[-1] * carry
-            x = (x + (pq[i, o, 1] + dup[c, here, span])) / den
+            x = (x + (pq[i, 2 * o + 1] + dup[c, here, span])) / den
             out[c, depth - 1, here, span] = x
             for k in reversed(range(depth - 1)):
                 rho = up(RHO, c, base + k)
@@ -436,8 +496,8 @@
         await_bytes(wrecv.at[0], sent.at[W_UP])
 
     if group > 1:
-        await_bytes(be.at[:, pl.ds(1, group - 1)], sent.at[PUSH])
-        await_bytes(ret.at[:, pl.ds(1, group - 1)], sent.at[GIVE])
+        await_edge(lambda size: be.at[:, pl.ds(0, size)], sent.at[PUSH])
+        await_lacking(lambda size: ret.at[:, pl.ds(0, size)], sent.at[GIVE])
     if count > 1:
         await_bytes(ztop, sent.at[ALONG_Z])
 
@@ -480,12 +540,12 @@
             vmem((comps, ny, nx)),
             vmem((comps, ny, nx)),
             vmem((comps, ny, nx)),
-            vmem((chunks, group, 2, part, piece)),
-            vmem((chunks, group, 2, part, piece)),
+            vmem((chunks, 2 * group, part, piece)),
+            vmem((chunks, 2 * group, part, piece)),
             vmem((chunks, 2, part, piece)),
             vmem((chunks, max(count - 1, 1), part, piece)),
-            vmem((chunks, group, 2, part, piece)),
-            vmem((chunks, group, 2, part, piece)),
+            vmem((chunks, 2 * group, part, piece)),
+            vmem((chunks, 2 * group, part, piece)),
             dma((3,)),
             pltpu.SemaphoreType.REGULAR((max(count - 1, 1),)),
             dma((6,)),

time: 37.4 us -> 35.5 us (0.949)
  Pallas kernels: 35.3 us -> 33.3 us
    pallas_call x1, Pallas kernels: 35.3 us -> 33.3 us  [shards(): pl.pallas_call(functools.partial(step_kernel, rows, cols, group, halves),...]
where the time goes in v4:
time: 35.5 us; the launch traced here: 35.4 us
  Pallas kernels  33.3 us (94%)
  local copies, waits for them, and re-layouts  2.02 us (6%)
    pallas_call x1, Pallas kernels, shards(): pl.pallas_call(functools.partial(step_kernel, rows, cols, group, halves),...  33.3 us
    unnamed x1, local copies, waits for them, and re-layouts  2.02 us

profile of v4, /device:TPU:0, one launch (start us, length us, event | category | flops | bytes accessed | tf_op | source)
XLA Modules:
  0.0 35.4 jit_solution(16925168668336947917)
XLA Ops:
  0.0 33.3 %convection_step.1 = f32[4,8,32,1024]{3,2,1,0:T(8,128)S(1)} custom-call(f32[4,8,32,1024]{3,2,1,0:T(8,128)} %state.1, f32[1,128]{1,0:T(1,128)} %bitcast.1, f32[4]{0:T(128)} %diffusivity.1), custom_call_target="tpu_custom_call" | custom-call | tf_op jit(solution)/shard_map/convection_step/pallas_call | solution.py:526
  33.3 2.0 %copy.5 = f32[4,8,32,1024]{3,2,1,0:T(8,128)} copy(f32[4,8,32,1024]{3,2,1,0:T(8,128)S(1)} %convection_step.1) | data formatting | bytes 8388608

commit v5 on v4

--- a/solution.py
+++ b/solution.py
@@ -12,7 +12,7 @@
 buoyancy = 1.0
 UNROLL = 8
 HALVES = 2
-LAG = 3
+LAG = 5
 MESH = pl.DeviceIdType.MESH
 
 PUSH, ALONG_Z, GIVE, Y_ROWS, W_UP, W_DOWN = range(6)
@@ -108,27 +108,39 @@
     def greet(device):
         pl.semaphore_signal(barrier, inc=1, device_id=device, device_id_type=MESH)
 
-    def await_ready(o, when):
+    def await_ready(index, when):
         @pl.when(when)
         def _():
-            pl.semaphore_wait(ready.at[o - 1], 1)
+            pl.semaphore_wait(ready.at[index], 1)
 
     def peer(o):
         return (g + o) % group
 
-    signal(barrier, me > 0, (jnp.maximum(me - 1, 0), col))
-    signal(barrier, me < rows - 1, (jnp.minimum(me + 1, rows - 1), col))
-    for o in range(1, group):
-        greet((z * group + peer(o), col))
+    even = g % 2 == 0
+    last = g == group - 1
+
+    def twin(o):
+        return jnp.where(even, o == 1, o == group - 1)
+
+    if group > 1:
+        greet((z * group + g + jnp.where(even, 1, -1), col))
     sides = [nxt] if cols == 2 else [nxt, prv]
     for side in sides:
         greet((me, side))
+    for o in range(1, group):
+        signal(barrier, (g + o < group) & ~twin(o), (z * group + peer(o), col))
     for o in range(1, count):
         signal(barrier, z + o < count, (jnp.minimum(z + o, count - 1) * group + g, col))
-    greetings = group - 1 + len(sides) + z
-    greetings = greetings + jnp.minimum(me, 1) + jnp.minimum(rows - 1 - me, 1)
-
+    greetings = len(sides) + z
+    if group > 1:
+        greetings = greetings + g + jnp.where(even, 1, 0)
     pl.semaphore_wait(barrier, greetings)
+
+    along_z = group - 1
+    for o in range(1, count):
+        signal(ready.at[along_z + o], z - o >= 0, (jnp.maximum(z - o, 0) * group + g, col))
+    for o in range(1, group):
+        signal(ready.at[group - o], (g + o >= group) & ~twin(o), (z * group + peer(o), col))
 
     def remote(src, dst, kind, sem, device):
         return pltpu.make_async_remote_copy(
@@ -163,24 +175,28 @@
             (jnp.minimum(me + 1, rows - 1), col),
         )
 
-    for h in range(halves):
-
-        @pl.when(me > 0)
-        def _(h=h):
-            w_down(h).start()
-
-        @pl.when(me < rows - 1)
-        def _(h=h):
-            w_up(h).start()
-
-    for o in range(1, count):
-        signal(ready.at[o - 1], z - o >= 0, (jnp.maximum(z - o, 0) * group + g, col))
+    def send_w(way, when):
+        @pl.when(when & ((me < rows - 1) if way else (me > 0)))
+        def _():
+            for h in range(halves):
+                (w_up if way else w_down)(h).start()
+
+    send_w(0, g > 0)
+    send_w(1, even & ~last)
 
     for copy in takes:
         copy.wait()
     fill_tables(depth, thick, diff, vtab)
     publish = pltpu.make_async_copy(vtab, tab, small.at[2])
     publish.start()
+
+    if group > 1:
+        await_ready(1, ~even & ~last)
+        await_ready(group - 1, (g == 0) & (z > 0) & ~twin(group - 1))
+    if count > 1:
+        await_ready(along_z + 1, last & (z < count - 1))
+    send_w(1, ~even | last)
+    send_w(0, g == 0)
 
     def y_copies(c):
         return [
@@ -242,12 +258,11 @@
     def z_slot(o, way):
         return count - o - 1 if way == 0 else o - 1
 
-    def give(i, o, way=None):
-        to = peer(o)
+    def give(i, to, way=None):
         first, size = (0, 2) if way is None else (way, 1)
         return remote(
             ret.at[i, pl.ds(2 * to + first, size)],
-            pq.at[i, pl.ds(2 * (group - o) + first, size)],
+            pq.at[i, pl.ds(2 * slot(to) + first, size)],
             GIVE,
             s3.at[i],
             (z * group + to, col),
@@ -362,6 +377,9 @@
                 be[i, 2 * p, local, :] = b[:, p * piece : (p + 1) * piece]
                 be[i, 2 * p + 1, local, :] = e[:, p * piece : (p + 1) * piece]
         for o in range(1, group):
+            if i == 0:
+                heard = ((o == 1) & ~even) | ((o == group - 1) & (g == 0) & (z > 0))
+                await_ready(o, (g + o < group) & ~twin(o) & ~heard)
             start_of(functools.partial(push, i, o), me, 0)
         for way in range(2):
             got[i, way] = be[i, 2 * g + way]
@@ -394,6 +412,23 @@
         if group > 1:
             await_lacking(lambda size: got.at[i, pl.ds(2, size)], s1.at[i])
 
+        if i == 0:
+            for o in range(1, count):
+                await_ready(along_z + o, (z + o < count) & ~(last & (o == 1)))
+
+        @pl.when(z > 0)
+        def _():
+            total = got[i, 2 * slot(group - 1) + 1]
+            for j in reversed(range(group - 1)):
+                total = got[i, 2 * slot(j) + 1] + down_factor(c, z * group + j) * total
+            top[i, 1] = total
+
+        for o in reversed(range(1, count)):
+
+            @pl.when(z - o >= 0)
+            def _(o=o):
+                send_z(i, o, 1).start()
+
         @pl.when(z < count - 1)
         def _():
             total = got[i, 2 * slot(0)]
@@ -401,24 +436,11 @@
                 total = got[i, 2 * slot(j)] + up_factor(c, z * group + j) * total
             top[i, 0] = total
 
-        @pl.when(z > 0)
-        def _():
-            total = got[i, 2 * slot(group - 1) + 1]
-            for j in reversed(range(group - 1)):
-                total = got[i, 2 * slot(j) + 1] + down_factor(c, z * group + j) * total
-            top[i, 1] = total
-
-        for o in range(1, count):
-            if i == 0:
-                await_ready(o, z + o < count)
+        for o in reversed(range(1, count)):
 
             @pl.when(z + o < count)
             def _(o=o):
                 send_z(i, o, 0).start()
-
-            @pl.when(z - o >= 0)
-            def _(o=o):
-                send_z(i, o, 1).start()
 
     def scatter(i):
         c = chunks[i][0]
@@ -448,8 +470,12 @@
             ret[i, 2 * j + 1] = carry
             if j > 0:
                 carry = got[i, 2 * slot(j) + 1] + down_factor(c, z * group + j) * carry
-        for o in range(1, group):
-            start_of(functools.partial(give, i, o), z * group + peer(o), 1)
+        for to in range(group):
+
+            @pl.when(g != to)
+            def _(to=to):
+                start_of(functools.partial(give, i, to), z * group + to, 1)
+
         for way in range(2):
             pq[i, way] = ret[i, 2 * g + way]
 
@@ -547,7 +573,7 @@
             vmem((chunks, 2 * group, part, piece)),
             vmem((chunks, 2 * group, part, piece)),
             dma((3,)),
-            pltpu.SemaphoreType.REGULAR((max(count - 1, 1),)),
+            pltpu.SemaphoreType.REGULAR((group + count,)),
             dma((6,)),
             dma,
             dma,

time: 35.5 us -> 34.5 us (0.972)
  Pallas kernels: 33.3 us -> 32.3 us
    pallas_call x1, Pallas kernels: 33.3 us -> 32.3 us  [shards(): pl.pallas_call(functools.partial(step_kernel, rows, cols, group, halves),...]
where the time goes in v5:
time: 34.5 us; the launch traced here: 34.3 us
  Pallas kernels  32.3 us (94%)
  local copies, waits for them, and re-layouts  2.02 us (6%)
    pallas_call x1, Pallas kernels, shards(): pl.pallas_call(functools.partial(step_kernel, rows, cols, group, halves),...  32.3 us
    unnamed x1, local copies, waits for them, and re-layouts  2.02 us

profile of v5, /device:TPU:0, one launch (start us, length us, event | category | flops | bytes accessed | tf_op | source)
XLA Modules:
  0.0 34.3 jit_solution(8001916731275590508)
XLA Ops:
  0.0 32.3 %convection_step.1 = f32[4,8,32,1024]{3,2,1,0:T(8,128)S(1)} custom-call(f32[4,8,32,1024]{3,2,1,0:T(8,128)} %state.1, f32[1,128]{1,0:T(1,128)} %bitcast.1, f32[4]{0:T(128)} %diffusivity.1), custom_call_target="tpu_custom_call" | custom-call | tf_op jit(solution)/shard_map/convection_step/pallas_call | solution.py:552
  32.3 2.0 %copy.5 = f32[4,8,32,1024]{3,2,1,0:T(8,128)} copy(f32[4,8,32,1024]{3,2,1,0:T(8,128)S(1)} %convection_step.1) | data formatting | bytes 8388608

commit v6 on v5

--- a/solution.py
+++ b/solution.py
@@ -95,9 +95,6 @@
         pltpu.make_async_copy(spacing, thick, small.at[0]),
         pltpu.make_async_copy(diffusivity, diff, small.at[1]),
     ]
-    for copy in takes + loads:
-        copy.start()
-
     barrier = pltpu.get_barrier_semaphore()
 
     def signal(sem, when, device):
@@ -131,6 +128,9 @@
         signal(barrier, (g + o < group) & ~twin(o), (z * group + peer(o), col))
     for o in range(1, count):
         signal(barrier, z + o < count, (jnp.minimum(z + o, count - 1) * group + g, col))
+    for copy in takes + loads:
+        copy.start()
+
     greetings = len(sides) + z
     if group > 1:
         greetings = greetings + g + jnp.where(even, 1, 0)
@@ -264,7 +264,7 @@
             ret.at[i, pl.ds(2 * to + first, size)],
             pq.at[i, pl.ds(2 * slot(to) + first, size)],
             GIVE,
-            s3.at[i],
+            s3.at[i if i < len(chunks) - 1 else i + slot(to) - 1],
             (z * group + to, col),
         )
 
@@ -285,14 +285,14 @@
     lacking = jnp.where((z == 0) & (g > 0), 1, 0)
     lacking = lacking + jnp.where((z == count - 1) & (g < group - 1), 1, 0)
 
-    def await_edge(refs, sem):
+    def await_edge(refs, sem, partners):
         @pl.when(at_edge)
         def _():
-            await_bytes(refs(group - 1), sem)
+            await_bytes(refs(partners), sem)
 
         @pl.when(jnp.logical_not(at_edge))
         def _():
-            await_bytes(refs(2 * (group - 1)), sem)
+            await_bytes(refs(2 * partners), sem)
 
     def await_lacking(refs, sem):
         for lacks in range(2 if count > 1 else 3):
@@ -487,10 +487,13 @@
             pis.append(pis[-1] * up(LAM, c, base + k))
         end = base + depth - 1
         den = up(GEE, c, end) + up(UPPER, c, end) * down(QSH, c, end)
-        if group > 1:
-            await_edge(lambda size: pq.at[i, pl.ds(0, size)], s3.at[i])
-        for o in range(group):
+        final = i == len(chunks) - 1
+        if group > 1 and not final:
+            await_edge(lambda size: pq.at[i, pl.ds(0, size)], s3.at[i], group - 1)
+        for o in sorted(range(group), key=lambda o: (o > 0, o % 2)):
             p = peer(o)
+            if o and final:
+                await_edge(lambda size: pq.at[i, pl.ds(2 * o, size)], s3.at[i + o - 1], 1)
             span = pl.ds(pl.multiple_of(p * piece, piece), piece)
             carry = pq[i, 2 * o] + ploc[c, here, span]
             x = out[c, depth - 1, here, span] + pis[-1] * carry
@@ -506,9 +509,13 @@
         gather(i)
         if i >= LAG:
             scatter(i - LAG)
+    settled = 0
     for i in range(max(total_chunks - LAG, 0), total_chunks):
         scatter(i)
-    for i in range(total_chunks):
+        if i >= total_chunks - 2:
+            settle(settled)
+            settled += 1
+    for i in range(settled, total_chunks):
         settle(i)
 
     await_bytes(ysend, sent.at[Y_ROWS])
@@ -522,7 +529,7 @@
         await_bytes(wrecv.at[0], sent.at[W_UP])
 
     if group > 1:
-        await_edge(lambda size: be.at[:, pl.ds(0, size)], sent.at[PUSH])
+        await_edge(lambda size: be.at[:, pl.ds(0, size)], sent.at[PUSH], group - 1)
         await_lacking(lambda size: ret.at[:, pl.ds(0, size)], sent.at[GIVE])
     if count > 1:
         await_bytes(ztop, sent.at[ALONG_Z])
@@ -573,14 +580,14 @@
             vmem((chunks, 2 * group, part, piece)),
             vmem((chunks, 2 * group, part, piece)),
             dma((3,)),
-            pltpu.SemaphoreType.REGULAR((group + count,)),
+            pltpu.SemaphoreType.REGULAR((max(group + count - 1, 1),)),
             dma((6,)),
             dma,
             dma,
             dma((2, halves)),
             dma((chunks,)),
             dma((chunks,)),
-            dma((chunks,)),
+            dma((chunks - 1 + max(group - 1, 1),)),
         ],
         compiler_params=pltpu.CompilerParams(
             collective_id=0, has_side_effects=True, vmem_limit_bytes=46 << 20

time: 34.5 us -> 34.5 us (level)
  no operation moved by 1% of the time
where the time goes in v6:
time: 34.5 us; the launch traced here: 34.3 us
  Pallas kernels  32.3 us (94%)
  local copies, waits for them, and re-layouts  2.02 us (6%)
    pallas_call x1, Pallas kernels, shards(): pl.pallas_call(functools.partial(step_kernel, rows, cols, group, halves),...  32.3 us
    unnamed x1, local copies, waits for them, and re-layouts  2.02 us

profile of v6, /device:TPU:0, one launch (start us, length us, event | category | flops | bytes accessed | tf_op | source)
XLA Modules:
  0.0 34.3 jit_solution(17256528946592720293)
XLA Ops:
  0.0 32.3 %convection_step.1 = f32[4,8,32,1024]{3,2,1,0:T(8,128)S(1)} custom-call(f32[4,8,32,1024]{3,2,1,0:T(8,128)} %state.1, f32[1,128]{1,0:T(1,128)} %bitcast.1, f32[4]{0:T(128)} %diffusivity.1), custom_call_target="tpu_custom_call" | custom-call | tf_op jit(solution)/shard_map/convection_step/pallas_call | solution.py:559
  32.3 2.0 %copy.5 = f32[4,8,32,1024]{3,2,1,0:T(8,128)} copy(f32[4,8,32,1024]{3,2,1,0:T(8,128)S(1)} %convection_step.1) | data formatting | bytes 8388608

commit v7 on v6

--- a/solution.py
+++ b/solution.py
@@ -184,12 +184,6 @@
     send_w(0, g > 0)
     send_w(1, even & ~last)
 
-    for copy in takes:
-        copy.wait()
-    fill_tables(depth, thick, diff, vtab)
-    publish = pltpu.make_async_copy(vtab, tab, small.at[2])
-    publish.start()
-
     if group > 1:
         await_ready(1, ~even & ~last)
         await_ready(group - 1, (g == 0) & (z > 0) & ~twin(group - 1))
@@ -213,6 +207,12 @@
     for c in range(comps):
         for copy in y_copies(c):
             copy.start()
+
+    for copy in takes:
+        copy.wait()
+    fill_tables(depth, thick, diff, vtab)
+    publish = pltpu.make_async_copy(vtab, tab, small.at[2])
+    publish.start()
 
     @pl.when(me == 0)
     def _():

time: 34.5 us -> 34.5 us (level)
  no operation moved by 1% of the time
where the time goes in v7:
time: 34.5 us; the launch traced here: 34.4 us
  Pallas kernels  32.4 us (94%)
  local copies, waits for them, and re-layouts  2.02 us (6%)
    pallas_call x1, Pallas kernels, shards(): pl.pallas_call(functools.partial(step_kernel, rows, cols, group, halves),...  32.4 us
    unnamed x1, local copies, waits for them, and re-layouts  2.02 us

profile of v7, /device:TPU:0, one launch (start us, length us, event | category | flops | bytes accessed | tf_op | source)
XLA Modules:
  0.0 34.4 jit_solution(1849516706230522261)
XLA Ops:
  0.0 32.4 %convection_step.1 = f32[4,8,32,1024]{3,2,1,0:T(8,128)S(1)} custom-call(f32[4,8,32,1024]{3,2,1,0:T(8,128)} %state.1, f32[1,128]{1,0:T(1,128)} %bitcast.1, f32[4]{0:T(128)} %diffusivity.1), custom_call_target="tpu_custom_call" | custom-call | tf_op jit(solution)/shard_map/convection_step/pallas_call | solution.py:559
  32.4 2.0 %copy.5 = f32[4,8,32,1024]{3,2,1,0:T(8,128)} copy(f32[4,8,32,1024]{3,2,1,0:T(8,128)S(1)} %convection_step.1) | data formatting | bytes 8388608
